TPU v7x, 32 devices: a whole 2x2x4 slice. The times are simulated.
32 devices in a mesh: band: 8 (over y, x, core), bus: 4 (over z).
Axes of the slice: x: 2, y: 2, z: 4, core: 2. Of those that a mesh axis runs over, the one named last changes fastest.
Arguments:
- dispatch0: float32 [64, 5120], P(None, ('band', 'bus')), may hold values from 0 to 1
- cost_lin: float32 [5120], P(('band', 'bus')), may hold values from -1 to 1
- cost_quad: float32 [5120], P(('band', 'bus')), may hold values from 0.5 to 4
- gen_max: float32 [5120], P(('band', 'bus')), may hold values from 0.5 to 2
- bus_map: int32 [5120], P(('band', 'bus')), may hold values from 0 to 98303, as said below
- demand: float32 [64, 4, 24576], P(None, 'bus', 'band'), may hold values from -6 to 6
- ptdf: float32 [2048, 98304], P('band', 'bus'), may hold values from -0.01953125 to 0.01953125
- line_price0: float32 [64, 2048], P(None, 'band'), may hold values from -3 to 3
- flow_max: float32 [2048], P('band'), may hold values from 0.3 to 3
Outputs:
- dispatch: float32 [64, 5120], P(None, ('band', 'bus'))
- line_price: float32 [64, 2048], P(None, 'band')
Inputs may be any that keep to these rules, and one draw needn't show every extreme that they name: `bus_map`: call bus 24576 * j + 3072 * i + k with 0 <= k < 3072 a bus of sub-block (i, j). Among the 160 generators of one aligned block (generators 160 * d to 160 * d + 159), at most 6 are sited in one sub-block, and one sub-block holds exactly 6 generators of every block.
All inputs are finite; a program needn't handle non-finite values.
Results may differ from a plain program's by a relative error of at most 0.0003.
Values sent between devices are 32-bit elements; how exact they have to be, the bound alone decides.
A program may use at most 128 MiB of HBM per device.

v0:
```python
import jax
import jax.numpy as jnp
from jax import lax
from jax.sharding import PartitionSpec as P

ITERS = 2
primal_step = 0.5
dual_step = 1.0


def owner_slots(bus_map, bus_width, sub_width, bus_count, slot_cap):
    block = bus_map // bus_width
    within = bus_map % bus_width
    owner = within // sub_width * bus_count + block
    local = within % sub_width
    same = owner[:, None] == owner[None, :]
    earlier = lax.broadcasted_iota(jnp.int32, same.shape, 0) > lax.broadcasted_iota(
        jnp.int32, same.shape, 1
    )
    rank = jnp.sum((same & earlier).astype(jnp.int32), axis=1)
    return (owner * slot_cap + rank, local)


def pack_rows(values, target, total):
    return jnp.zeros((total, values.shape[1]), values.dtype).at[target].set(values)


def on_device(
    dispatch0, cost_lin, cost_quad, gen_max, bus_map, demand, ptdf, line_price0, flow_max
):
    band_count = lax.axis_size("band")
    bus_count = lax.axis_size("bus")
    owner_count = band_count * bus_count
    gen_count = bus_map.shape[0]
    slot_cap = (gen_count + owner_count - 1) // owner_count + 1
    total = owner_count * slot_cap
    scenarios = dispatch0.shape[0]
    sub_width = demand.shape[2]
    bus_width = ptdf.shape[1]
    target, local = owner_slots(bus_map, bus_width, sub_width, bus_count, slot_cap)
    site_code = (local + 1).astype(jnp.float32)
    load = demand[:, 0, :]
    line_price = line_price0
    dispatch = dispatch0
    code_out = pack_rows(site_code[:, None], target, total).reshape(owner_count, slot_cap)
    column_ids = None
    for iteration in range(ITERS):
        sent = pack_rows(dispatch.T, target, total).reshape(owner_count, slot_cap * scenarios)
        arrived, codes = (
            lax.all_to_all(sent, ("band", "bus"), split_axis=0, concat_axis=0, tiled=True),
            lax.all_to_all(code_out, ("band", "bus"), split_axis=0, concat_axis=0, tiled=True),
        )
        slot_local = jnp.maximum(codes.reshape(total) - 1.0, 0.0).astype(jnp.int32)
        spread = (
            jnp.zeros((sub_width, scenarios), jnp.float32)
            .at[slot_local]
            .add(arrived.reshape(total, scenarios))
        )
        injection = spread.T - load
        flow = lax.psum(
            lax.dot_general(
                lax.all_gather(injection, "band", axis=1, tiled=True),
                ptdf,
                (((1,), (1,)), ((), ())),
                precision=lax.Precision.HIGHEST,
                preferred_element_type=jnp.float32,
            ),
            "bus",
        )
        bound = dual_step * flow_max
        trial = line_price + dual_step * flow
        price_next = trial - jnp.clip(trial, -bound, bound)
        line_price, reflected = (price_next, 2.0 * price_next - line_price)
        if iteration == 0:
            gathered = lax.all_gather(slot_local, "band", axis=0, tiled=True)
            position = lax.broadcasted_iota(jnp.int32, gathered.shape, 0)
            column_ids = position // total * sub_width + gathered
        rows_columns = jnp.take(ptdf, column_ids, axis=1)
        slot_price = lax.psum_scatter(
            lax.dot_general(
                rows_columns,
                reflected,
                (((0,), (1,)), ((), ())),
                precision=lax.Precision.HIGHEST,
                preferred_element_type=jnp.float32,
            ),
            "band",
            scatter_dimension=0,
            tiled=True,
        )
        answer = slot_price.reshape(owner_count, slot_cap * scenarios)
        back = lax.all_to_all(answer, ("band", "bus"), split_axis=0, concat_axis=0, tiled=True)
        unit_price = back.reshape(total, scenarios)[target].T
        dispatch = jnp.clip(
            (dispatch - primal_step * (cost_lin[None, :] + unit_price))
            / (1.0 + primal_step * cost_quad[None, :]),
            0.0,
            gen_max[None, :],
        )
    return (dispatch, line_price)


def solution(mesh):
    in_specs = (
        P(None, ("band", "bus")),
        P(("band", "bus")),
        P(("band", "bus")),
        P(("band", "bus")),
        P(("band", "bus")),
        P(None, "bus", "band"),
        P("band", "bus"),
        P(None, "band"),
        P("band"),
    )
    out_specs = (P(None, ("band", "bus")), P(None, "band"))
    return jax.shard_map(
        on_device, mesh=mesh, in_specs=in_specs, out_specs=out_specs, check_vma=False
    )
```

profile of v0, /device:TPU:0, one launch (start us, length us, event | category | flops | bytes accessed | tf_op | source)
XLA Modules:
  0.0 428.0 jit_solution(5949450486282528453)
XLA Ops:
  7.2 0.7 fusion.39
  7.9 0.2 convert_reduce_fusion
  8.1 1.1 scatter_custom_fusion
  9.2 0.7 all_to_all.31
  9.9 7.3 %all-to-all-start = ((f32[32,1,6]{2,1,0:T(1,128)}), f32[32,1,6]{2,1,0:T(1,128)S(1)}, u32[]{:S(2)}, u32[]{:S(2)}) async-start(f32[32,1,6]{2,1,0:T(1,128)} %bitcast), calls=%async_computation | async-start | bytes 32768 | tf_op jit(solution)/shard_map/all_to_all | solution.py:51
  17.3 2.3 copy.38
  19.6 0.1 copy.36
  19.7 1.0 scatter_custom_fusion.1
  20.7 0.7 all_to_all.41
  21.4 3.0 all-to-all-done
  24.4 2.9 all-to-all-start.1
  27.3 0.0 all-gather.3.cloned.1.call-start
  27.4 0.1 convert_element_type.27
  27.5 7.2 %all-to-all-done.1 = f32[32,1,384]{2,1,0:T(1,128)S(1)} async-done(((f32[32,1,384]{2,1,0:T(1,128)}), f32[32,1,384]{2,1,0:T(1,128)S(1)}, u32[]{:S(2)}, u32[]{:S(2)}) %all-to-all-start.1) | async-done | bytes 49184 | tf_op jit(solution)/shard_map/all_to_all | solution.py:50
  34.7 0.1 reduce.2
  34.8 0.1 reshape.143
  34.9 1.6 scatter_custom_fusion.2
  36.5 1.3 bitcast_subtract_fusion.1
  37.8 0.0 all-gather.3.cloned.1.call-update
  37.8 0.0 all-reduce.4.cloned.1.call-start
  37.9 25.0 %copy.35 = f32[256,24576]{0,1:T(8,128)} copy(f32[256,24576]{1,0:T(8,128)} %param.17) | data formatting | bytes 50331648 | tf_op args[6]
  62.9 0.6 dynamic-slice
  64.1 0.1 fusion.46
  64.2 0.1 reshape.171
  64.3 0.3 dynamic-update-slice
  64.6 6.6 %all-reduce = s32[1536]{0:T(1024)S(1)} all-reduce(s32[1536]{0:T(1024)S(1)} %dynamic-update-slice), channel_id=1, replica_groups=mesh['band'=8,'bus'=4] {'band'}, use_global_device_ids=true, to_apply=%add | all-reduce | flops 1536 | bytes 12288
  71.2 35.3 %all-gather.3.cloned.1.call-done = f32[64,24576]{0,1:T(8,128)} async-done(((f32[64,3072]{0,1:T(8,128)}), f32[64,24576]{0,1:T(8,128)}) %all-gather.3.cloned.1.call-update) | async-done | bytes 6291472 | tf_op jit(solution)/shard_map/all_gather | solution.py:62
  106.5 27.7 %fusion.48 = f32[64,256]{1,0:T(8,128)} fusion(f32[64,24576]{0,1:T(8,128)} %all-gather.3.cloned.1.call-done, f32[256,24576]{1,0:T(8,128)} %param.17), kind=kOutput, calls=%fused_computation.81 | convolution fusion | flops 4831838208 | bytes 31522816 | tf_op jit(solution)/shard_map/dot_general | solution.py:61
  134.2 0.3 reduce-scatter.7.cloned.1.call-start
  134.5 11.9 %gather_fusion.2 = f32[1536,256]{1,0:T(8,128)S(1)} fusion(f32[256,24576]{0,1:T(8,128)} %copy.35, s32[2048]{0:T(1024)S(1)} %pad_clamp_fusion), kind=kCustom, calls=%fused_computation.clone | custom fusion | bytes 3151872 | tf_op jit(solution)/shard_map/jit(_take)/gather | solution.py:78
  146.4 22.2 %all-reduce.4.cloned.1.call-done = f32[64,256]{1,0:T(8,128)} async-done(((f32[64,256]{1,0:T(8,128)}), f32[64,256]{1,0:T(8,128)}) %all-reduce.4.cloned.1.call-update) | async-done | bytes 65552 | tf_op jit(solution)/shard_map/psum | solution.py:60
  168.6 3.2 fusion.2
  171.8 0.0 reduce-scatter.7.cloned.1.call-update
  171.8 0.1 copy.41
  171.9 34.7 %reduce-scatter.7.cloned.1.call-done = f32[192,64]{1,0:T(8,128)} async-done(((f32[1536,64]{1,0:T(8,128)}), f32[192,64]{1,0:T(8,128)}) %reduce-scatter.7.cloned.1.call-update) | async-done | bytes 49168 | tf_op jit(solution)/shard_map/reduce_scatter | solution.py:79
  206.6 1.6 all_to_all.42
  208.2 4.6 %all-to-all-start.2 = ((f32[32,1,384]{2,1,0:T(1,128)}), f32[32,1,384]{2,1,0:T(1,128)S(1)}, u32[]{:S(2)}, u32[]{:S(2)}) async-start(f32[32,1,384]{2,1,0:T(1,128)} %all_to_all.42), calls=%async_computation.2 | async-start | bytes 98304 | tf_op jit(solution)/shard_map/all_to_all | solution.py:92
  212.8 0.0 all-gather.5.cloned.1.call-start
  212.9 7.3 %all-to-all-done.2 = f32[32,1,384]{2,1,0:T(1,128)S(1)} async-done(((f32[32,1,384]{2,1,0:T(1,128)}), f32[32,1,384]{2,1,0:T(1,128)S(1)}, u32[]{:S(2)}, u32[]{:S(2)}) %all-to-all-start.2) | async-done | bytes 49184 | tf_op jit(solution)/shard_map/all_to_all | solution.py:92
  220.2 0.1 reduce.3
  220.3 0.1 reshape.94
  220.4 0.7 gather_fusion
  221.1 1.1 scatter_custom_fusion.3
  222.2 0.1 all_to_all.43
  222.3 9.1 %all_to_all.50 = f32[32,1,384]{2,1,0:T(1,128)S(1)} all-to-all(f32[32,1,384]{2,1,0:T(1,128)S(1)} %all_to_all.43), channel_id=1, replica_groups=mesh['band'=8,'bus'=4] {'band','bus'}, dimensions={0} | all-to-all | bytes 98304 | tf_op jit(solution)/shard_map/all_to_all | solution.py:50
  231.4 0.1 reduce.4
  231.5 0.7 reshape.159
  232.2 2.8 scatter_custom_fusion.4
  235.1 2.8 bitcast_subtract_fusion
  237.9 0.0 all-reduce.6.cloned.1.call-start
  237.9 68.5 %all-gather.5.cloned.1.call-done = f32[64,24576]{0,1:T(8,128)} async-done(((f32[64,3072]{0,1:T(8,128)}), f32[64,24576]{0,1:T(8,128)}) %all-gather.5.cloned.1.call-update) | async-done | bytes 6291472 | tf_op jit(solution)/shard_map/all_gather | solution.py:62
  306.4 27.7 %fusion.49 = f32[64,256]{1,0:T(8,128)} fusion(f32[64,24576]{0,1:T(8,128)} %all-gather.5.cloned.1.call-done, f32[256,24576]{1,0:T(8,128)} %param.17), kind=kOutput, calls=%fused_computation.82 | convolution fusion | flops 4831838208 | bytes 31522816 | tf_op jit(solution)/shard_map/dot_general | solution.py:61
  334.1 0.0 reduce-scatter.9.cloned.1.call-start
  334.2 34.4 %all-reduce.6.cloned.1.call-done = f32[64,256]{1,0:T(8,128)} async-done(((f32[64,256]{1,0:T(8,128)}), f32[64,256]{1,0:T(8,128)}) %all-reduce.6.cloned.1.call-update) | async-done | bytes 65552 | tf_op jit(solution)/shard_map/psum | solution.py:60
  368.6 0.9 minimum_subtract_fusion
  369.5 2.3 fusion
  371.8 34.8 %reduce-scatter.9.cloned.1.call-done = f32[192,64]{1,0:T(8,128)} async-done(((f32[1536,64]{1,0:T(8,128)}), f32[192,64]{1,0:T(8,128)}) %reduce-scatter.9.cloned.1.call-update) | async-done | bytes 49168 | tf_op jit(solution)/shard_map/reduce_scatter | solution.py:79
  406.6 1.0 all_to_all.44
  407.6 11.8 %all_to_all.51 = f32[32,1,384]{2,1,0:T(1,128)S(1)} all-to-all(f32[32,1,384]{2,1,0:T(1,128)S(1)} %all_to_all.44), channel_id=1, replica_groups=mesh['band'=8,'bus'=4] {'band','bus'}, dimensions={0} | all-to-all | bytes 98304 | tf_op jit(solution)/shard_map/all_to_all | solution.py:92
  419.5 0.1 reduce.5
  419.6 0.1 reshape.96
  419.7 0.7 gather_fusion.1
  420.3 0.1 fusion.17
  420.5 0.7 copy.45
  (33 shorter events, 0.2 us)
Async XLA Ops:
  7.2 12.4 %copy-start.2 = (f32[64,160]{1,0:T(8,128)S(1)}, f32[64,160]{1,0:T(8,128)}, u32[]{:S(2)}) copy-start(f32[64,160]{1,0:T(8,128)} %param.11) | copy-start | bytes 122884
  9.9 14.5 %all-to-all-start = ((f32[32,1,6]{2,1,0:T(1,128)}), f32[32,1,6]{2,1,0:T(1,128)S(1)}, u32[]{:S(2)}, u32[]{:S(2)}) async-start(f32[32,1,6]{2,1,0:T(1,128)} %bitcast), calls=%async_computation | async-start | bytes 32768 | tf_op jit(solution)/shard_map/all_to_all | solution.py:51
  24.4 10.3 %all-to-all-start.1 = ((f32[32,1,384]{2,1,0:T(1,128)}), f32[32,1,384]{2,1,0:T(1,128)S(1)}, u32[]{:S(2)}, u32[]{:S(2)}) async-start(f32[32,1,384]{2,1,0:T(1,128)} %all_to_all.41), calls=%async_computation.1 | async-start | bytes 98304 | tf_op jit(solution)/shard_map/all_to_all | solution.py:50
  27.3 79.2 %all-gather.3.cloned.1.call-start = ((), (), s32[]{:S(2)}) async-start(), calls=%async_computation.7 | async-start | bytes 14155776 | tf_op jit(solution)/shard_map/all_gather | solution.py:62
  27.5 10.3 %copy-start.8 = (s32[192,1]{0,1:T(1,128)}, s32[192,1]{0,1:T(1,128)S(1)}, u32[]{:S(2)}) copy-start(s32[192,1]{0,1:T(1,128)S(1)} %compare_select_fusion.1) | copy-start | bytes 2308
  37.8 130.8 %all-reduce.4.cloned.1.call-start = ((), (), s32[]{:S(2)}) async-start(), calls=%async_computation.8 | async-start | bytes 131072 | tf_op jit(solution)/shard_map/psum | solution.py:60
  37.9 25.0 %copy-start.4 = (f32[256]{0:T(256)S(1)}, f32[256]{0:T(256)}, u32[]{:S(2)}) copy-start(f32[256]{0:T(256)} %param.19) | copy-start | bytes 3076
  37.9 25.0 %copy-start.9 = (u32[32]{0:T(128)S(1)}, u32[32]{0:T(128)}, u32[]{:S(2)}) copy-start(u32[32]{0:T(128)} %constant.80) | copy-start | bytes 388
  134.2 72.3 %reduce-scatter.7.cloned.1.call-start = ((), (), s32[]{:S(2)}) async-start(), calls=%async_computation.11 | async-start | bytes 884736 | tf_op jit(solution)/shard_map/reduce_scatter | solution.py:79
  134.5 34.1 %copy-start = (f32[64,256]{1,0:T(8,128)S(1)}, f32[64,256]{1,0:T(8,128)}, u32[]{:S(2)}) copy-start(f32[64,256]{1,0:T(8,128)} %param.18) | copy-start | bytes 196612
  168.6 3.3 copy-start.7
  171.8 49.3 %copy-start.5 = (f32[160]{0:T(256)S(1)}, f32[160]{0:T(256)}, u32[]{:S(2)}) copy-start(f32[160]{0:T(256)} %param.12) | copy-start | bytes 1924
  171.8 49.3 %copy-start.6 = (f32[160]{0:T(256)S(1)}, f32[160]{0:T(256)}, u32[]{:S(2)}) copy-start(f32[160]{0:T(256)} %param.14) | copy-start | bytes 1924
  208.2 12.0 %all-to-all-start.2 = ((f32[32,1,384]{2,1,0:T(1,128)}), f32[32,1,384]{2,1,0:T(1,128)S(1)}, u32[]{:S(2)}, u32[]{:S(2)}) async-start(f32[32,1,384]{2,1,0:T(1,128)} %all_to_all.42), calls=%async_computation.2 | async-start | bytes 98304 | tf_op jit(solution)/shard_map/all_to_all | solution.py:92
  212.8 93.6 %all-gather.5.cloned.1.call-start = ((), (), s32[]{:S(2)}) async-start(), calls=%async_computation.9 | async-start | bytes 14155776 | tf_op jit(solution)/shard_map/all_gather | solution.py:62
  237.9 130.8 %copy-start.1 = (f32[64,256]{1,0:T(8,128)S(1)}, f32[64,256]{1,0:T(8,128)}, u32[]{:S(2)}) copy-start(f32[64,256]{1,0:T(8,128)} %all-reduce.4.cloned.1.call-done) | copy-start | bytes 196612
  237.9 130.7 %all-reduce.6.cloned.1.call-start = ((), (), s32[]{:S(2)}) async-start(), calls=%async_computation.10 | async-start | bytes 131072 | tf_op jit(solution)/shard_map/psum | solution.py:60
  334.1 72.5 %reduce-scatter.9.cloned.1.call-start = ((), (), s32[]{:S(2)}) async-start(), calls=%async_computation.12 | async-start | bytes 884736 | tf_op jit(solution)/shard_map/reduce_scatter | solution.py:79
  369.5 2.4 copy-start.3
Sparse Core Ops, SparseCore 0:
  37.9 68.5 all-gather.2
  134.3 34.2 all-reduce.3
  171.9 34.6 reduce-scatter.6
  238.0 68.4 all-gather.4
  334.3 34.2 all-reduce.5
  371.9 34.6 reduce-scatter.8
where the time goes:
time: 429 us; the launch traced here: 428 us
  waiting for transfers between devices  247 us (58%)
  matrix products  60.9 us (14%)
  local copies, waits for them, and re-layouts  49.7 us (12%)
  blocking collectives  27.5 us (6%)
  starting transfers between devices  15.3 us (4%)
  between operations  15.1 us (4%)
  other arithmetic  12.1 us (3%)
    all_gather x2, waiting for transfers between devices, on_device(): lax.all_gather(injection, 'band', axis=1, tiled=True)  104 us
    reduce_scatter x2, waiting for transfers between devices, on_device(): lax.psum_scatter(lax.dot_general(rows_columns, reflected, (((0,), (1,)),...  69.5 us
    psum x2, waiting for transfers between devices, on_device(): lax.psum(lax.dot_general(lax.all_gather(injection, 'band', axis=1, tiled=...  56.6 us
    dot_general x2, matrix products, on_device(): lax.dot_general(lax.all_gather(injection, 'band', axis=1, tiled=True), pt...  55.4 us
    unnamed x26, local copies, waits for them, and re-layouts  29 us
    gather x1, local copies, waits for them, and re-layouts, on_device(): rows_columns = jnp.take(ptdf, column_ids, axis=1)  11.9 us
    all_to_all x1, blocking collectives, on_device(): lax.all_to_all(answer, ('band', 'bus'), split_axis=0, concat_axis=0, tile...  11.8 us
    all_to_all x1, blocking collectives, on_device(): lax.all_to_all(sent, ('band', 'bus'), split_axis=0, concat_axis=0, tiled=...  9.09 us
  transfers between devices with their start and end apart: 9, of which 9 were waited for; matrix products, arithmetic and copies ran while one was open for 10% of the time, Pallas kernels for 0%

commit v1 on v0

--- a/solution.py
+++ b/solution.py
@@ -6,6 +6,28 @@
 ITERS = 2
 primal_step = 0.5
 dual_step = 1.0
+
+
+def joined_along(parts, dim):
+    shape = list(parts.shape[1:])
+    shape[dim] *= parts.shape[0]
+    return jnp.moveaxis(parts, 0, dim).reshape(shape)
+
+
+def collected_by_bits(value, axis):
+    size = lax.axis_size(axis)
+    blocks = value[None]
+    for level in range(size.bit_length() - 1):
+        apart = 1 << level
+        partner_block = lax.ppermute(blocks, axis, [(i, i ^ apart) for i in range(size)])
+        both = jnp.stack([blocks, partner_block])
+        upper = lax.axis_index(axis) >> level & 1
+        blocks = jnp.where(upper == 0, both, both[::-1]).reshape(-1, *value.shape)
+    return blocks
+
+
+def gather_by_bits(value, axis, dim):
+    return joined_along(collected_by_bits(value, axis), dim)
 
 
 def owner_slots(bus_map, bus_width, sub_width, bus_count, slot_cap):
@@ -59,7 +81,7 @@
         injection = spread.T - load
         flow = lax.psum(
             lax.dot_general(
-                lax.all_gather(injection, "band", axis=1, tiled=True),
+                gather_by_bits(injection, "band", 1),
                 ptdf,
                 (((1,), (1,)), ((), ())),
                 precision=lax.Precision.HIGHEST,

time: 429 us -> 571 us (1.33)
  local copies, waits for them, and re-layouts: 49.7 us -> 94.5 us
  blocking collectives: 27.5 us -> 63.6 us
  other arithmetic: 12.1 us -> 43.4 us
  waiting for transfers between devices: 247 us -> 275 us
    ppermute x0 -> x6, waiting for transfers between devices: none -> 139 us  [collected_by_bits(): lax.ppermute(blocks, axis, [(i, i ^ apart) for i in range(size)])]
    all_gather x2 -> x0, waiting for transfers between devices: 104 us -> none  [on_device(): lax.all_gather(injection, 'band', axis=1, tiled=True)]
    unnamed x1, blocking collectives: 6.56 us -> 42.6 us
    another operation x0 -> x10, other arithmetic: none -> 27.5 us  [collected_by_bits(): both = jnp.stack([blocks, partner_block])]
    reshape x0 -> x4, local copies, waits for them, and re-layouts: none -> 16.9 us  [collected_by_bits(): blocks = jnp.where(upper == 0, both, both[::-1]).reshape(-1, *value.shape)]
    another operation x0 -> x2, local copies, waits for them, and re-layouts: none -> 12.2 us  [collected_by_bits(): both = jnp.stack([blocks, partner_block])]
    ppermute x0 -> x4, local copies, waits for them, and re-layouts: none -> 9.81 us  [collected_by_bits(): lax.ppermute(blocks, axis, [(i, i ^ apart) for i in range(size)])]
    select_n x0 -> x4, other arithmetic: none -> 7.89 us  [collected_by_bits(): blocks = jnp.where(upper == 0, both, both[::-1]).reshape(-1, *value.shape)]
  transfers between devices with their start and end apart: 9 -> 13, of which waited for: 9 -> 12; matrix products, arithmetic and copies ran while one was open for 10% -> 10% of each run, Pallas kernels for 0% -> 0%
where the time goes in v1:
time: 571 us; the launch traced here: 570 us
  waiting for transfers between devices  275 us (48%)
  local copies, waits for them, and re-layouts  94.5 us (17%)
  blocking collectives  63.6 us (11%)
  matrix products  59.3 us (10%)
  other arithmetic  43.4 us (8%)
  starting transfers between devices  18.7 us (3%)
  between operations  14.9 us (3%)
    ppermute x6, waiting for transfers between devices, collected_by_bits(): lax.ppermute(blocks, axis, [(i, i ^ apart) for i in range(size)])  139 us
    reduce_scatter x2, waiting for transfers between devices, on_device(): lax.psum_scatter(lax.dot_general(rows_columns, reflected, (((0,), (1,)),...  69.4 us
    dot_general x2, matrix products, on_device(): lax.dot_general(gather_by_bits(injection, 'band', 1), ptdf, (((1,), (1,))...  53.8 us
    psum x2, waiting for transfers between devices, on_device(): lax.psum(lax.dot_general(gather_by_bits(injection, 'band', 1), ptdf, (((1...  49.9 us
    unnamed x1, blocking collectives  42.6 us
    unnamed x28, local copies, waits for them, and re-layouts  30.2 us
    another operation x10, other arithmetic, collected_by_bits(): both = jnp.stack([blocks, partner_block])  27.5 us
    reshape x4, local copies, waits for them, and re-layouts, collected_by_bits(): blocks = jnp.where(upper == 0, both, both[::-1]).reshape(-1, *value.shape)  16.9 us
  transfers between devices with their start and end apart: 13, of which 12 were waited for; matrix products, arithmetic and copies ran while one was open for 10% of the time, Pallas kernels for 0%

profile of v1, /device:TPU:0, one launch (start us, length us, event | category | flops | bytes accessed | tf_op | source)
XLA Modules:
  0.0 569.7 jit_solution(786574872112724597)
XLA Ops:
  8.1 1.1 scatter_custom_fusion
  9.9 7.3 %all-to-all-start = ((f32[32,1,6]{2,1,0:T(1,128)}), f32[32,1,6]{2,1,0:T(1,128)S(1)}, u32[]{:S(2)}, u32[]{:S(2)}) async-start(f32[32,1,6]{2,1,0:T(1,128)} %bitcast), calls=%async_computation | async-start | bytes 32768 | tf_op jit(solution)/shard_map/all_to_all | solution.py:73
  17.2 2.3 copy.59
  19.6 0.9 copy.57
  20.5 1.0 scatter_custom_fusion.1
  21.5 0.7 all_to_all.41
  22.2 2.1 all-to-all-done
  24.3 3.7 all-to-all-start.1
  28.3 7.2 %all-to-all-done.1 = f32[32,1,384]{2,1,0:T(1,128)S(1)} async-done(((f32[32,1,384]{2,1,0:T(1,128)}), f32[32,1,384]{2,1,0:T(1,128)S(1)}, u32[]{:S(2)}, u32[]{:S(2)}) %all-to-all-start.1) | async-done | bytes 49184 | tf_op jit(solution)/shard_map/all_to_all | solution.py:72
  35.7 1.6 scatter_custom_fusion.2
  37.3 1.9 fusion.19
  39.2 1.9 copy.60
  41.1 2.4 collective-permute-done
  43.5 1.6 copy.61
  45.1 1.6 pad_maximum_fusion.4
  46.7 3.1 fusion.1
  49.8 2.3 copy.63
  52.8 35.9 %collective-permute-done.1 = f32[2,64,3072]{2,1,0:T(8,128)} collective-permute-done((f32[2,64,3072]{2,1,0:T(8,128)S(1)}, f32[2,64,3072]{2,1,0:T(8,128)}, u32[]{:S(2)}, u32[]{:S(2)}) %collective-permute-start.1) | collective-permute-done | bytes 1572896 | tf_op jit(solution)/shard_map/ppermute | solution.py:22
  88.8 3.3 copy.64
  92.1 3.3 pad_maximum_fusion
  95.3 3.1 reverse_select_fusion.3
  98.4 6.1 %copy.65 = f32[4,64,3072]{2,1,0:T(8,128)} copy(f32[4,64,3072]{1,2,0:T(8,128)} %bitcast.107) | data formatting | bytes 6291456 | tf_op jit(solution)/shard_map/reshape | solution.py:25
  105.2 24.7 %copy.56 = f32[256,24576]{0,1:T(8,128)} copy(f32[256,24576]{1,0:T(8,128)} %param.17) | data formatting | bytes 50331648 | tf_op args[6]
  131.6 42.6 %all-reduce = s32[1536]{0:T(1024)S(1)} all-reduce(s32[1536]{0:T(1024)S(1)} %dynamic-update-slice), channel_id=1, replica_groups=mesh['band'=8,'bus'=4] {'band'}, use_global_device_ids=true, to_apply=%add | all-reduce | flops 1536 | bytes 12288
  174.3 6.1 %copy.66 = f32[1,4,64,3072]{3,2,1,0:T(8,128)} copy(f32[1,4,64,3072]{2,3,1,0:T(8,128)} %bitcast.108) | data formatting | bytes 6291456 | tf_op jit(solution)/shard_map/stack;reshape | solution.py:23
  180.4 3.3 pad_maximum_fusion.1
  183.7 0.8 reverse_select_fusion.2
  184.5 0.7 copy.86
  185.3 26.9 %fusion.56 = f32[64,256]{1,0:T(8,128)} fusion(f32[64,24576]{1,0:T(8,128)S(1)} %bitcast.113, f32[256,24576]{1,0:T(8,128)} %param.17), kind=kOutput, calls=%fused_computation.101 | convolution fusion | flops 4831838208 | bytes 31522816 | tf_op jit(solution)/shard_map/dot_general | solution.py:83
  212.3 11.9 %gather_fusion.2 = f32[1536,256]{1,0:T(8,128)S(1)} fusion(f32[256,24576]{0,1:T(8,128)} %copy.56, s32[2048]{0:T(1024)S(1)} %pad_clamp_fusion), kind=kCustom, calls=%fused_computation.clone | custom fusion | bytes 3151872 | tf_op jit(solution)/shard_map/jit(_take)/gather | solution.py:100
  224.2 19.1 %all-reduce.4.cloned.1.call-done = f32[64,256]{1,0:T(8,128)} async-done(((f32[64,256]{1,0:T(8,128)}), f32[64,256]{1,0:T(8,128)}) %all-reduce.4.cloned.1.call-update) | async-done | bytes 65552 | tf_op jit(solution)/shard_map/psum | solution.py:82
  243.3 3.1 fusion.6
  246.6 34.6 %reduce-scatter.7.cloned.1.call-done = f32[192,64]{1,0:T(8,128)} async-done(((f32[1536,64]{1,0:T(8,128)}), f32[192,64]{1,0:T(8,128)}) %reduce-scatter.7.cloned.1.call-update) | async-done | bytes 49168 | tf_op jit(solution)/shard_map/reduce_scatter | solution.py:101
  281.2 1.6 all_to_all.42
  282.9 4.6 all-to-all-start.2
  287.5 7.3 %all-to-all-done.2 = f32[32,1,384]{2,1,0:T(1,128)S(1)} async-done(((f32[32,1,384]{2,1,0:T(1,128)}), f32[32,1,384]{2,1,0:T(1,128)S(1)}, u32[]{:S(2)}, u32[]{:S(2)}) %all-to-all-start.2) | async-done | bytes 49184 | tf_op jit(solution)/shard_map/all_to_all | solution.py:114
  295.8 1.1 scatter_custom_fusion.3
  297.0 9.1 %all_to_all.50 = f32[32,1,384]{2,1,0:T(1,128)S(1)} all-to-all(f32[32,1,384]{2,1,0:T(1,128)S(1)} %all_to_all.43), channel_id=1, replica_groups=mesh['band'=8,'bus'=4] {'band','bus'}, dimensions={0} | all-to-all | bytes 98304 | tf_op jit(solution)/shard_map/all_to_all | solution.py:72
  306.9 2.8 scatter_custom_fusion.4
  309.7 3.3 fusion.21
  313.0 1.9 copy.72
  314.9 2.4 collective-permute-done.3
  317.3 1.6 copy.73
  318.9 1.6 pad_maximum_fusion.5
  320.5 3.1 fusion.3
  323.6 2.3 copy.74
  326.7 35.9 %collective-permute-done.4 = f32[2,64,3072]{2,1,0:T(8,128)} collective-permute-done((f32[2,64,3072]{2,1,0:T(8,128)S(1)}, f32[2,64,3072]{2,1,0:T(8,128)}, u32[]{:S(2)}, u32[]{:S(2)}) %collective-permute-start.4) | collective-permute-done | bytes 1572896 | tf_op jit(solution)/shard_map/ppermute | solution.py:22
  362.6 3.3 copy.75
  365.9 3.3 pad_maximum_fusion.2
  369.1 3.1 reverse_select_fusion.1
  372.2 6.1 %copy.76 = f32[4,64,3072]{2,1,0:T(8,128)} copy(f32[4,64,3072]{1,2,0:T(8,128)} %bitcast.109) | data formatting | bytes 6291456 | tf_op jit(solution)/shard_map/reshape | solution.py:25
  379.0 6.1 %copy.77 = f32[1,4,64,3072]{3,2,1,0:T(8,128)} copy(f32[1,4,64,3072]{2,3,1,0:T(8,128)} %bitcast.110) | data formatting | bytes 6291456 | tf_op jit(solution)/shard_map/stack;reshape | solution.py:23
  385.1 62.8 %collective-permute-done.5 = f32[4,64,3072]{2,1,0:T(8,128)} collective-permute-done((f32[4,64,3072]{2,1,0:T(8,128)}, f32[4,64,3072]{2,1,0:T(8,128)}, u32[]{:S(2)}, u32[]{:S(2)}) %collective-permute-start.5) | collective-permute-done | bytes 3145760 | tf_op jit(solution)/shard_map/ppermute | solution.py:22
  447.9 3.3 pad_maximum_fusion.3
  451.2 0.8 reverse_select_fusion
  452.0 0.7 copy.87
  452.8 26.9 %fusion.57 = f32[64,256]{1,0:T(8,128)} fusion(f32[64,24576]{1,0:T(8,128)S(1)} %bitcast.114, f32[256,24576]{1,0:T(8,128)} %param.17), kind=kOutput, calls=%fused_computation.102 | convolution fusion | flops 4831838208 | bytes 31522816 | tf_op jit(solution)/shard_map/dot_general | solution.py:83
  479.8 30.8 %all-reduce.6.cloned.1.call-done = f32[64,256]{1,0:T(8,128)} async-done(((f32[64,256]{1,0:T(8,128)}), f32[64,256]{1,0:T(8,128)}) %all-reduce.6.cloned.1.call-update) | async-done | bytes 65552 | tf_op jit(solution)/shard_map/psum | solution.py:82
  510.6 0.9 minimum_subtract_fusion
  511.5 2.3 fusion.4
  513.8 34.8 %reduce-scatter.9.cloned.1.call-done = f32[192,64]{1,0:T(8,128)} async-done(((f32[1536,64]{1,0:T(8,128)}), f32[192,64]{1,0:T(8,128)}) %reduce-scatter.9.cloned.1.call-update) | async-done | bytes 49168 | tf_op jit(solution)/shard_map/reduce_scatter | solution.py:101
  548.6 1.0 all_to_all.44
  549.6 11.8 %all_to_all.51 = f32[32,1,384]{2,1,0:T(1,128)S(1)} all-to-all(f32[32,1,384]{2,1,0:T(1,128)S(1)} %all_to_all.44), channel_id=1, replica_groups=mesh['band'=8,'bus'=4] {'band','bus'}, dimensions={0} | all-to-all | bytes 98304 | tf_op jit(solution)/shard_map/all_to_all | solution.py:114
  562.5 0.7 copy.81
  (65 shorter events, 9.0 us)
Async XLA Ops:
  9.9 14.5 %all-to-all-start = ((f32[32,1,6]{2,1,0:T(1,128)}), f32[32,1,6]{2,1,0:T(1,128)S(1)}, u32[]{:S(2)}, u32[]{:S(2)}) async-start(f32[32,1,6]{2,1,0:T(1,128)} %bitcast), calls=%async_computation | async-start | bytes 32768 | tf_op jit(solution)/shard_map/all_to_all | solution.py:73
  24.3 11.1 %all-to-all-start.1 = ((f32[32,1,384]{2,1,0:T(1,128)}), f32[32,1,384]{2,1,0:T(1,128)S(1)}, u32[]{:S(2)}, u32[]{:S(2)}) async-start(f32[32,1,384]{2,1,0:T(1,128)} %all_to_all.41), calls=%async_computation.1 | async-start | bytes 98304 | tf_op jit(solution)/shard_map/all_to_all | solution.py:72
  28.1 215.2 %all-reduce.4.cloned.1.call-start = ((), (), s32[]{:S(2)}) async-start(), calls=%async_computation.7 | async-start | bytes 131072 | tf_op jit(solution)/shard_map/psum | solution.py:82
  28.3 10.9 %copy-start.8 = (s32[192,1]{0,1:T(1,128)}, s32[192,1]{0,1:T(1,128)S(1)}, u32[]{:S(2)}) copy-start(s32[192,1]{0,1:T(1,128)S(1)} %compare_select_fusion.1) | copy-start | bytes 2308
  41.0 2.5 collective-permute-start
  52.1 36.6 %collective-permute-start.1 = (f32[2,64,3072]{2,1,0:T(8,128)S(1)}, f32[2,64,3072]{2,1,0:T(8,128)}, u32[]{:S(2)}, u32[]{:S(2)}) collective-permute-start(f32[2,64,3072]{2,1,0:T(8,128)S(1)} %copy.63), channel_id=1, source_target_pairs={{0,8},{4,12},{8,0},{12,4},{16,24},{20,28},{24,16},{28,20},{1,9},{5... | collective-permute-start | bytes 4718600 | tf_op jit(solution)/shard_map/ppermute | solution.py:22
  104.6 75.8 %collective-permute-start.2 = (f32[4,64,3072]{2,1,0:T(8,128)}, f32[4,64,3072]{2,1,0:T(8,128)}, u32[]{:S(2)}, u32[]{:S(2)}) collective-permute-start(f32[4,64,3072]{2,1,0:T(8,128)} %copy.65), channel_id=1, source_target_pairs={{0,16},{4,20},{8,24},{12,28},{16,0},{20,4},{24,8},{28,12},{1,17},{... | collective-permute-start | bytes 9437192 | tf_op jit(solution)/shard_map/ppermute | solution.py:22
  105.2 24.7 %copy-start.4 = (f32[256]{0:T(256)S(1)}, f32[256]{0:T(256)}, u32[]{:S(2)}) copy-start(f32[256]{0:T(256)} %param.19) | copy-start | bytes 3076
  105.2 24.7 %copy-start.9 = (u32[32]{0:T(128)S(1)}, u32[32]{0:T(128)}, u32[]{:S(2)}) copy-start(u32[32]{0:T(128)} %constant.89) | copy-start | bytes 388
  212.2 69.0 %reduce-scatter.7.cloned.1.call-start = ((), (), s32[]{:S(2)}) async-start(), calls=%async_computation.9 | async-start | bytes 884736 | tf_op jit(solution)/shard_map/reduce_scatter | solution.py:101
  212.3 31.0 %copy-start = (f32[64,256]{1,0:T(8,128)S(1)}, f32[64,256]{1,0:T(8,128)}, u32[]{:S(2)}) copy-start(f32[64,256]{1,0:T(8,128)} %param.18) | copy-start | bytes 196612
  224.2 22.3 %copy-start.2 = (f32[64,160]{1,0:T(8,128)S(1)}, f32[64,160]{1,0:T(8,128)}, u32[]{:S(2)}) copy-start(f32[64,160]{1,0:T(8,128)} %param.11) | copy-start | bytes 122884
  224.2 22.4 %copy-start.7 = (f32[160]{0:T(256)S(1)}, f32[160]{0:T(256)}, u32[]{:S(2)}) copy-start(f32[160]{0:T(256)} %param.13) | copy-start | bytes 1924
  224.2 71.6 %copy-start.5 = (f32[160]{0:T(256)S(1)}, f32[160]{0:T(256)}, u32[]{:S(2)}) copy-start(f32[160]{0:T(256)} %param.12) | copy-start | bytes 1924
  224.2 71.5 %copy-start.6 = (f32[160]{0:T(256)S(1)}, f32[160]{0:T(256)}, u32[]{:S(2)}) copy-start(f32[160]{0:T(256)} %param.14) | copy-start | bytes 1924
  282.9 12.0 %all-to-all-start.2 = ((f32[32,1,384]{2,1,0:T(1,128)}), f32[32,1,384]{2,1,0:T(1,128)S(1)}, u32[]{:S(2)}, u32[]{:S(2)}) async-start(f32[32,1,384]{2,1,0:T(1,128)} %all_to_all.42), calls=%async_computation.2 | async-start | bytes 98304 | tf_op jit(solution)/shard_map/all_to_all | solution.py:114
  287.5 223.1 %all-reduce.6.cloned.1.call-start = ((), (), s32[]{:S(2)}) async-start(), calls=%async_computation.8 | async-start | bytes 131072 | tf_op jit(solution)/shard_map/psum | solution.py:82
  314.8 2.5 collective-permute-start.3
  326.0 36.6 %collective-permute-start.4 = (f32[2,64,3072]{2,1,0:T(8,128)S(1)}, f32[2,64,3072]{2,1,0:T(8,128)}, u32[]{:S(2)}, u32[]{:S(2)}) collective-permute-start(f32[2,64,3072]{2,1,0:T(8,128)S(1)} %copy.74), channel_id=1, source_target_pairs={{0,8},{4,12},{8,0},{12,4},{16,24},{20,28},{24,16},{28,20},{1,9},{5... | collective-permute-start | bytes 4718600 | tf_op jit(solution)/shard_map/ppermute | solution.py:22
  378.3 69.6 %collective-permute-start.5 = (f32[4,64,3072]{2,1,0:T(8,128)}, f32[4,64,3072]{2,1,0:T(8,128)}, u32[]{:S(2)}, u32[]{:S(2)}) collective-permute-start(f32[4,64,3072]{2,1,0:T(8,128)} %copy.76), channel_id=1, source_target_pairs={{0,16},{4,20},{8,24},{12,28},{16,0},{20,4},{24,8},{28,12},{1,17},{... | collective-permute-start | bytes 9437192 | tf_op jit(solution)/shard_map/ppermute | solution.py:22
  452.8 57.8 %copy-start.1 = (f32[64,256]{1,0:T(8,128)S(1)}, f32[64,256]{1,0:T(8,128)}, u32[]{:S(2)}) copy-start(f32[64,256]{1,0:T(8,128)} %all-reduce.4.cloned.1.call-done) | copy-start | bytes 196612
  479.7 68.9 %reduce-scatter.9.cloned.1.call-start = ((), (), s32[]{:S(2)}) async-start(), calls=%async_computation.10 | async-start | bytes 884736 | tf_op jit(solution)/shard_map/reduce_scatter | solution.py:101
  511.5 51.7 %copy-start.3 = (f32[64,256]{1,0:T(8,128)}, f32[64,256]{1,0:T(8,128)S(1)}, u32[]{:S(2)}) copy-start(f32[64,256]{1,0:T(8,128)S(1)} %minimum_subtract_fusion) | copy-start | bytes 196612
Sparse Core Ops, SparseCore 0:
  212.3 30.9 all-reduce.3
  246.6 34.6 reduce-scatter.6
  479.9 30.6 all-reduce.5
  514.0 34.6 reduce-scatter.8
